TPU v7x, 512 devices: a whole 4x4x16 slice. The times are simulated.
512 devices in a mesh: dom: 16 (over z), feat: 32 (over x, y, core).
Axes of the slice: x: 4, y: 4, z: 16, core: 2. Of those that a mesh axis runs over, the one named last changes fastest.
Arguments:
- node_feats: bfloat16 [1024, 65536], P('feat', 'dom'), may hold values from -6 to 6
- out_cotangent: bfloat16 [1024, 65536], P('feat', 'dom'), may hold values from -6 to 6
- weight_self: bfloat16 [1024, 1024], P('feat'), may hold values from -0.1875 to 0.1875
- weight_neigh: bfloat16 [1024, 1024], P('feat'), may hold values from -1.5 to 1.5
- out_bias: float32 [1024], P('feat'), may hold values from -3 to 3
- send_blocks: int32 [16, 16, 2], P('dom'), may hold values from 0 to 31
- tile_rows: int32 [16, 64], P('dom'), may hold values from 0 to 31
- tile_cols: int32 [16, 64], P('dom'), may hold values from 0 to 63
- tile_count: int32 [16], P('dom'), may hold values from 1 to 64, as said below
- tile_values: bfloat16 [16, 64, 128, 128], P('dom'), may hold values from 0 to 1
Outputs:
- layer_out: bfloat16 [1024, 65536], P('feat', 'dom')
- feats_grad: bfloat16 [1024, 65536], P('feat', 'dom')
- grad_self: float32 [1024, 1024], P('feat')
- grad_neigh: float32 [1024, 1024], P('feat')
- grad_bias: float32 [1024], P('feat')
Inputs may be any that keep to these rules, and one draw needn't show every extreme that they name: Slots t >= tile_count[p] of tile_rows, tile_cols and tile_values are not part of the graph; some partition uses all 64 slots.
All inputs are finite; a program needn't handle non-finite values.
Results may differ from a plain program's by a relative error of at most 0.0075.
Values may be sent and summed in bfloat16 or wider, within the bound.
No kernel may reach another device: no remote copies, remote signals or barrier semaphores. Data moves between devices by JAX's collectives and lax.ppermute only.
A program may use at most 64 MiB of HBM per device.

v0:
```python
import jax
import jax.numpy as jnp
from jax import lax
from jax.sharding import PartitionSpec as P

BLK = 128
NBLK = 32
CAP = 2
TMAX = 64
ROWS = 4096


def gelu_tanh(values):
    return jax.nn.gelu(values, approximate=True)


def left_product(weights, data):
    return lax.dot_general(
        weights, data, (((0,), (0,)), ((), ())), preferred_element_type=jnp.float32
    )


def per_device(
    node_feats,
    out_cotangent,
    weight_self,
    weight_neigh,
    out_bias,
    send_blocks,
    tile_rows,
    tile_cols,
    tile_count,
    tile_values,
):
    highest = lax.Precision.HIGHEST
    local_width = node_feats.shape[0]
    num_parts = lax.axis_size("dom")
    ext_blocks = NBLK + num_parts * CAP
    my_sends = send_blocks[0].reshape(num_parts * CAP)
    my_rows = tile_rows[0]
    my_cols = tile_cols[0]
    my_tiles = tile_values[0]
    live = (jnp.arange(TMAX, dtype=jnp.int32) < tile_count[0]).astype(jnp.float32)
    blocks = node_feats.reshape(local_width, NBLK, BLK)
    outgoing = blocks[:, my_sends].reshape(local_width, num_parts * CAP * BLK)
    incoming = lax.all_to_all(outgoing, "dom", split_axis=1, concat_axis=1, tiled=True)
    extended = jnp.concatenate(
        [blocks, incoming.reshape(local_width, num_parts * CAP, BLK)], axis=1
    )
    rows_hot = jax.nn.one_hot(my_rows, NBLK, dtype=jnp.float32) * live[:, None]
    picked = extended[:, my_cols]
    products = jnp.einsum("ftc,trc->ftr", picked, my_tiles, preferred_element_type=jnp.float32)
    summed = jnp.einsum("ftr,tb->fbr", products, rows_hot, precision=highest)
    degree = jnp.einsum(
        "tr,tb->br", jnp.sum(my_tiles, axis=-1, dtype=jnp.float32), rows_hot, precision=highest
    )
    divisor = jnp.maximum(degree, 1.0)
    aggregate = (summed / divisor[None]).astype(jnp.bfloat16).reshape(local_width, ROWS)
    feat_rows, agg_rows = (
        lax.all_to_all(node_feats, "feat", split_axis=1, concat_axis=0, tiled=True),
        lax.all_to_all(aggregate, "feat", split_axis=1, concat_axis=0, tiled=True),
    )
    totals = left_product(lax.all_gather(weight_self, "feat", axis=0, tiled=True), feat_rows)
    out_by_rows = totals + left_product(
        lax.all_gather(weight_neigh, "feat", axis=0, tiled=True), agg_rows
    )
    pre_act = lax.all_to_all(out_by_rows, "feat", split_axis=0, concat_axis=1, tiled=True)
    pre_act = pre_act + out_bias[:, None]
    layer_out = gelu_tanh(pre_act).astype(jnp.bfloat16)
    grad_pre = jax.vjp(gelu_tanh, pre_act)[1](out_cotangent.astype(jnp.float32))[0].astype(
        jnp.bfloat16
    )
    shard_piece = lax.all_gather(grad_pre, "feat", axis=0, tiled=True)
    self_term = lax.dot_general(
        node_feats, shard_piece, (((1,), (1,)), ((), ())), preferred_element_type=jnp.float32
    )
    neigh_term = lax.dot_general(
        aggregate, shard_piece, (((1,), (1,)), ((), ())), preferred_element_type=jnp.float32
    )
    grad_w_self = self_term
    grad_w_neigh = neigh_term
    self_back = jnp.dot(weight_self, shard_piece, preferred_element_type=jnp.float32)
    neigh_back = jnp.dot(weight_neigh, shard_piece, preferred_element_type=jnp.float32)
    grad_w_self, grad_w_neigh, self_grad, neigh_back = (
        grad_w_self,
        grad_w_neigh,
        self_back,
        neigh_back,
    )
    agg_grad = neigh_back.reshape(local_width, NBLK, BLK) / divisor[None]
    bias_term = jnp.sum(grad_pre, axis=1, dtype=jnp.float32)
    grad_w_self, grad_w_neigh, bias_total = lax.psum((grad_w_self, grad_w_neigh, bias_term), "dom")
    scale = 1.0 / jnp.sqrt(jnp.float32(ROWS * num_parts))
    grad_self = grad_w_self * scale
    grad_neigh = grad_w_neigh * scale
    grad_bias = bias_total * scale
    picked_grad = agg_grad[:, my_rows]
    contrib = jnp.einsum(
        "ftr,trc->ftc", picked_grad, my_tiles.astype(jnp.float32), precision=highest
    )
    cols_hot = jax.nn.one_hot(my_cols, ext_blocks, dtype=jnp.float32) * live[:, None]
    ext_grad = jnp.einsum("ftc,tn->fnc", contrib, cols_hot, precision=highest)
    halo_grad = ext_grad[:, NBLK:].reshape(local_width, num_parts * CAP * BLK)
    returned = lax.all_to_all(halo_grad, "dom", split_axis=1, concat_axis=1, tiled=True)
    send_hot = jax.nn.one_hot(my_sends, NBLK, dtype=jnp.float32)
    gathered_back = jnp.einsum(
        "fsc,sb->fbc",
        returned.reshape(local_width, num_parts * CAP, BLK),
        send_hot,
        precision=highest,
    )
    total = self_grad.reshape(local_width, NBLK, BLK) + ext_grad[:, :NBLK] + gathered_back
    feats_grad = total.astype(jnp.bfloat16).reshape(local_width, ROWS)
    return (layer_out, feats_grad, grad_self, grad_neigh, grad_bias)


def solution(mesh):
    in_specs = (
        P("feat", "dom"),
        P("feat", "dom"),
        P("feat", None),
        P("feat", None),
        P("feat"),
        P("dom", None, None),
        P("dom", None),
        P("dom", None),
        P("dom"),
        P("dom", None, None, None),
    )
    out_specs = (P("feat", "dom"), P("feat", "dom"), P("feat", None), P("feat", None), P("feat"))
    return jax.shard_map(
        per_device, mesh=mesh, in_specs=in_specs, out_specs=out_specs, check_vma=False
    )
```

profile of v0, /device:TPU:2, one launch (start us, length us, event | category | flops | bytes accessed | tf_op | source)
XLA Modules:
  0.0 411.8 jit_solution(10953175642827898887)
XLA Ops:
  8.7 0.8 copy.39
  10.3 1.5 gather_fusion
  12.1 0.8 copy.42
  12.9 15.2 %all-to-all-start.1 = ((bf16[32,16,256]{2,0,1:T(8,128)(2,1)}), bf16[32,16,256]{2,0,1:T(8,128)(2,1)S(1)}, u32[]{:S(2)}, u32[]{:S(2)}) async-start(bf16[32,16,256]{2,0,1:T(8,128)(2,1)} %copy.42), calls=%async_computation.1 | async-start | bytes 524288 | tf_op jit(solution)/shard_map/all_to_all | solution.py:46
  29.6 16.9 %all-to-all-done.1 = bf16[32,16,256]{2,0,1:T(8,128)(2,1)S(1)} async-done(((bf16[32,16,256]{2,0,1:T(8,128)(2,1)}), bf16[32,16,256]{2,0,1:T(8,128)(2,1)S(1)}, u32[]{:S(2)}, u32[]{:S(2)}) %all-to-all-start.1) | async-done | bytes 262176 | tf_op jit(solution)/shard_map/all_to_all | solution.py:46
  46.5 7.7 %all-to-all-start = ((bf16[32,32,128]{2,0,1:T(8,128)(2,1)}), bf16[32,32,128]{2,0,1:T(8,128)(2,1)}, u32[]{:S(2)}, u32[]{:S(2)}) async-start(bf16[32,32,128]{2,0,1:T(8,128)(2,1)} %copy_bitcast_fusion.1), calls=%async_computation | async-start | bytes 524288 | tf_op jit(solution)/shard_map/all_to_all | solution.py:60
  54.5 1.0 pad_maximum_fusion
  56.2 1.2 fusion.4
  57.4 1.2 fusion.12
  59.3 0.8 copy.47
  60.1 1.8 all-to-all-done
  61.9 5.6 %all-to-all-start.2 = ((bf16[32,32,128]{2,0,1:T(8,128)(2,1)}), bf16[32,32,128]{2,0,1:T(8,128)(2,1)S(1)}, u32[]{:S(2)}, u32[]{:S(2)}) async-start(bf16[32,32,128]{2,0,1:T(8,128)(2,1)} %copy.47), calls=%async_computation.2 | async-start | bytes 524288 | tf_op jit(solution)/shard_map/all_to_all | solution.py:61
  67.6 7.1 %all-gather.4.cloned.1.call-done = bf16[1024,1024]{1,0:T(8,128)(2,1)} async-done(((bf16[32,1024]{1,0:T(8,128)(2,1)}), bf16[1024,1024]{1,0:T(8,128)(2,1)}) %all-gather.4.cloned.1.call-update) | async-done | bytes 2097168 | tf_op jit(solution)/shard_map/all_gather | solution.py:63
  74.7 2.3 fusion.54
  77.1 60.3 %all-gather.6.cloned.1.call-done = bf16[1024,1024]{1,0:T(8,128)(2,1)} async-done(((bf16[32,1024]{1,0:T(8,128)(2,1)}), bf16[1024,1024]{1,0:T(8,128)(2,1)}) %all-gather.6.cloned.1.call-update) | async-done | bytes 2097168 | tf_op jit(solution)/shard_map/all_gather | solution.py:65
  137.4 2.6 fusion.10
  140.0 15.6 %all_to_all.72 = f32[32,32,128]{2,1,0:T(8,128)S(1)} all-to-all(f32[32,32,128]{2,1,0:T(8,128)S(1)} %bitcast.119), channel_id=1, replica_groups=mesh['dom'=16,'feat'=32] {'feat'}, dimensions={0} | all-to-all | bytes 1048576 | tf_op jit(solution)/shard_map/all_to_all | solution.py:67
  155.6 1.4 convert_reduce_fusion.1
  157.0 67.5 %all-gather.8.cloned.1.call-done = bf16[1024,4096]{1,0:T(8,128)(2,1)} async-done(((bf16[32,4096]{1,0:T(8,128)(2,1)}), bf16[1024,4096]{1,0:T(8,128)(2,1)}) %all-gather.8.cloned.1.call-update) | async-done | bytes 8388624 | tf_op jit(solution)/shard_map/all_gather | solution.py:73
  224.6 5.1 %convolution_bitcast_fusion.1 = f32[4,32,8,128]{3,2,1,0:T(8,128)S(1)} fusion(bf16[32,1024]{1,0:T(8,128)(2,1)S(1)} %copy-done.5, bf16[1024,4096]{1,0:T(8,128)(2,1)} %all-gather.8.cloned.1.call-done), kind=kOutput, calls=%fused_computation.11 | convolution fusion | flops 268435456 | bytes 8978432 | tf_op jit(solution)/shard_map/dot_general | solution.py:83
  230.4 1.5 convolution_bitcast_fusion.2
  232.0 1.7 gather_fusion.2
  233.7 3.0 fusion.7
  236.7 1.6 convolution_bitcast_fusion
  238.6 1.2 copy.53
  239.7 12.3 %all-to-all-start.4 = ((f32[32,16,256]{2,0,1:T(8,128)}), f32[32,16,256]{2,0,1:T(8,128)S(1)}, u32[]{:S(2)}, u32[]{:S(2)}) async-start(f32[32,16,256]{2,0,1:T(8,128)} %copy.53), calls=%async_computation.4 | async-start | bytes 1048576 | tf_op jit(solution)/shard_map/all_to_all | solution.py:104
  252.1 6.7 %convolution_bitcast_fusion.5 = f32[32,1024]{1,0:T(8,128)} fusion(bf16[1024,4096]{1,0:T(8,128)(2,1)} %all-gather.8.cloned.1.call-done, bf16[32,4096]{1,0:T(8,128)(2,1)S(1)} %copy-done), kind=kOutput, calls=%fused_computation.20 | convolution fusion | flops 268435456 | bytes 8781824 | tf_op jit(solution)/shard_map/dot_general | solution.py:74
  258.7 6.6 %fusion.28 = f32[32,1024]{1,0:T(8,128)} fusion(bf16[1024,4096]{1,0:T(8,128)(2,1)} %all-gather.8.cloned.1.call-done, bf16[4,8,32,128]{3,2,1,0:T(8,128)(2,1)S(1)} %bitcast.121), kind=kOutput, calls=%fused_computation.46 | convolution fusion | flops 268435456 | bytes 8781824 | tf_op jit(solution)/shard_map/dot_general | solution.py:77
  265.5 35.6 %psum.23 = f32[32]{0:T(128)S(1)} all-reduce(f32[32]{0:T(128)S(1)} %get-tuple-element.7), channel_id=1, replica_groups=mesh['dom'=16,'feat'=32] {'dom'}, use_global_device_ids=true, to_apply=%region_4.5 | all-reduce | flops 32 | bytes 256 | tf_op jit(solution)/shard_map/psum | solution.py:92
  301.6 100.5 %all-reduce.3.cloned.1.call-done = (f32[32,1024]{1,0:T(8,128)}, f32[32,1024]{1,0:T(8,128)}) async-done(((f32[32,1024]{1,0:T(8,128)}, f32[32,1024]{1,0:T(8,128)}), (f32[32,1024]{1,0:T(8,128)}, f32[32,1024]{1,0:T(8,128)})) %all-reduce.3.cloned.1.call-update) | async-done | bytes 262160 | tf_op jit(solution)/shard_map/psum | solution.py:92
  402.1 1.7 broadcast_multiply_fusion
  404.5 0.8 copy.85
  (58 shorter events, 7.5 us)
Async XLA Ops:
  7.2 2.4 copy-start
  7.2 21.6 %copy-start.10 = (s32[1,64]{1,0:T(1,128)S(1)}, s32[1,64]{1,0:T(1,128)}, u32[]{:S(2)}) copy-start(s32[1,64]{1,0:T(1,128)} %param.17) | copy-start | bytes 772
  7.2 21.6 %copy-start.2 = (bf16[1,64,128,128]{3,2,1,0:T(8,128)(2,1)S(1)}, bf16[1,64,128,128]{3,2,1,0:T(8,128)(2,1)}, u32[]{:S(2)}) copy-start(bf16[1,64,128,128]{3,2,1,0:T(8,128)(2,1)} %param.19) | copy-start | bytes 6291460
  7.2 67.5 %all-gather.4.cloned.1.call-start = ((), (), s32[]{:S(2)}) async-start(), calls=%async_computation.5 | async-start | bytes 2162688 | tf_op jit(solution)/shard_map/all_gather | solution.py:63
  7.9 129.5 %all-gather.6.cloned.1.call-start = ((), (), s32[]{:S(2)}) async-start(), calls=%async_computation.6 | async-start | bytes 2162688 | tf_op jit(solution)/shard_map/all_gather | solution.py:65
  11.9 17.5 %copy-start.9 = (s32[1,64]{1,0:T(1,128)S(1)}, s32[1,64]{1,0:T(1,128)}, u32[]{:S(2)}) copy-start(s32[1,64]{1,0:T(1,128)} %param.16) | copy-start | bytes 772
  12.9 33.6 %all-to-all-start.1 = ((bf16[32,16,256]{2,0,1:T(8,128)(2,1)}), bf16[32,16,256]{2,0,1:T(8,128)(2,1)S(1)}, u32[]{:S(2)}, u32[]{:S(2)}) async-start(bf16[32,16,256]{2,0,1:T(8,128)(2,1)} %copy.42), calls=%async_computation.1 | async-start | bytes 524288 | tf_op jit(solution)/shard_map/all_to_all | solution.py:46
  46.5 15.4 %all-to-all-start = ((bf16[32,32,128]{2,0,1:T(8,128)(2,1)}), bf16[32,32,128]{2,0,1:T(8,128)(2,1)}, u32[]{:S(2)}, u32[]{:S(2)}) async-start(bf16[32,32,128]{2,0,1:T(8,128)(2,1)} %copy_bitcast_fusion.1), calls=%async_computation | async-start | bytes 524288 | tf_op jit(solution)/shard_map/all_to_all | solution.py:60
  58.6 0.7 copy-start.3
  61.9 15.2 %all-to-all-start.2 = ((bf16[32,32,128]{2,0,1:T(8,128)(2,1)}), bf16[32,32,128]{2,0,1:T(8,128)(2,1)S(1)}, u32[]{:S(2)}, u32[]{:S(2)}) async-start(bf16[32,32,128]{2,0,1:T(8,128)(2,1)} %copy.47), calls=%async_computation.2 | async-start | bytes 524288 | tf_op jit(solution)/shard_map/all_to_all | solution.py:61
  67.5 157.1 %all-gather.8.cloned.1.call-start = ((), (), s32[]{:S(2)}) async-start(), calls=%async_computation.7 | async-start | bytes 8650752 | tf_op jit(solution)/shard_map/all_gather | solution.py:73
  137.4 18.2 %copy-start.7 = (bf16[32,4096]{1,0:T(8,128)(2,1)S(1)}, bf16[32,4096]{1,0:T(8,128)(2,1)}, u32[]{:S(2)}) copy-start(bf16[32,4096]{1,0:T(8,128)(2,1)} %param.11) | copy-start | bytes 786436
  137.4 18.2 %copy-start.8 = (f32[32]{0:T(128)S(1)}, f32[32]{0:T(128)}, u32[]{:S(2)}) copy-start(f32[32]{0:T(128)} %param.14) | copy-start | bytes 388
  140.0 84.6 %copy-start.5 = (bf16[32,1024]{1,0:T(8,128)(2,1)S(1)}, bf16[32,1024]{1,0:T(8,128)(2,1)}, u32[]{:S(2)}) copy-start(bf16[32,1024]{1,0:T(8,128)(2,1)} %param.13) | copy-start | bytes 196612
  157.0 72.7 %copy-start.6 = (bf16[32,1024]{1,0:T(8,128)(2,1)S(1)}, bf16[32,1024]{1,0:T(8,128)(2,1)}, u32[]{:S(2)}) copy-start(bf16[32,1024]{1,0:T(8,128)(2,1)} %param.12) | copy-start | bytes 196612
  224.6 5.8 %copy-start.1 = (bf16[1024,4096]{1,0:T(8,128)(2,1)S(1)}, bf16[1024,4096]{1,0:T(8,128)(2,1)}, u32[]{:S(2)}) copy-start(bf16[1024,4096]{1,0:T(8,128)(2,1)} %all-gather.8.cloned.1.call-done) | copy-start | bytes 25165828
  239.7 164.0 %all-to-all-start.4 = ((f32[32,16,256]{2,0,1:T(8,128)}), f32[32,16,256]{2,0,1:T(8,128)S(1)}, u32[]{:S(2)}, u32[]{:S(2)}) async-start(f32[32,16,256]{2,0,1:T(8,128)} %copy.53), calls=%async_computation.4 | async-start | bytes 1048576 | tf_op jit(solution)/shard_map/all_to_all | solution.py:104
  252.0 6.7 %copy-start.4 = (bf16[32,32,128]{2,0,1:T(8,128)(2,1)S(1)}, bf16[32,32,128]{2,0,1:T(8,128)(2,1)}, u32[]{:S(2)}) copy-start(bf16[32,32,128]{2,0,1:T(8,128)(2,1)} %copy-done.3) | copy-start | bytes 786436
  252.0 150.0 %all-reduce.3.cloned.1.call-start = ((), (), s32[]{:S(2)}) async-start(), calls=%async_computation.8 | async-start | bytes 524288 | tf_op jit(solution)/shard_map/psum | solution.py:92
Sparse Core Ops, SparseCore 0:
  11.1 63.5 all-gather.3
  77.9 59.4 all-gather.5
  157.1 67.4 all-gather.7
  265.5 136.5 all-reduce.2
where the time goes:
time: 413 us; the launch traced here: 412 us
  waiting for transfers between devices  256 us (62%)
  blocking collectives  51.2 us (12%)
  starting transfers between devices  40.9 us (10%)
  matrix products  32.3 us (8%)
  between operations  14.8 us (4%)
  local copies, waits for them, and re-layouts  11.6 us (3%)
  other arithmetic  5.43 us (1%)
    psum x1, waiting for transfers between devices, per_device(): lax.psum((grad_w_self, grad_w_neigh, bias_term), 'dom')  100 us
    all_gather x1, waiting for transfers between devices, per_device(): shard_piece = lax.all_gather(grad_pre, 'feat', axis=0, tiled=True)  67.5 us
    all_gather x1, waiting for transfers between devices, per_device(): lax.all_gather(weight_neigh, 'feat', axis=0, tiled=True)  60.3 us
    psum x1, blocking collectives, per_device(): lax.psum((grad_w_self, grad_w_neigh, bias_term), 'dom')  35.6 us
    all_to_all x1, waiting for transfers between devices, per_device(): lax.all_to_all(outgoing, 'dom', split_axis=1, concat_axis=1, tiled=True)  16.9 us
    all_to_all x1, blocking collectives, per_device(): lax.all_to_all(out_by_rows, 'feat', split_axis=0, concat_axis=1, tiled=True)  15.6 us
    all_to_all x1, starting transfers between devices, per_device(): lax.all_to_all(outgoing, 'dom', split_axis=1, concat_axis=1, tiled=True)  15.2 us
    all_to_all x1, starting transfers between devices, per_device(): lax.all_to_all(halo_grad, 'dom', split_axis=1, concat_axis=1, tiled=True)  12.3 us
  transfers between devices with their start and end apart: 8, of which 6 were waited for; matrix products, arithmetic and copies ran while one was open for 7% of the time, Pallas kernels for 0%

commit v1 on v0

--- a/solution.py
+++ b/solution.py
@@ -2,6 +2,7 @@
 import jax.numpy as jnp
 from jax import lax
 from jax.sharding import PartitionSpec as P
+from jax.lax import all_to_all, axis_size
 
 BLK = 128
 NBLK = 32
@@ -62,7 +63,10 @@
     )
     totals = left_product(lax.all_gather(weight_self, "feat", axis=0, tiled=True), feat_rows)
     out_by_rows = totals + left_product(
-        lax.all_gather(weight_neigh, "feat", axis=0, tiled=True), agg_rows
+        jnp.concatenate(
+            all_to_all(jnp.stack([weight_neigh] * axis_size("feat")), "feat", 0, 0), axis=0
+        ),
+        agg_rows,
     )
     pre_act = lax.all_to_all(out_by_rows, "feat", split_axis=0, concat_axis=1, tiled=True)
     pre_act = pre_act + out_bias[:, None]

time: 413 us -> 382 us (0.925)
  waiting for transfers between devices: 256 us -> 183 us
  blocking collectives: 51.2 us -> 100 us
  starting transfers between devices: 40.9 us -> 34 us
    all_gather x1 -> x0, waiting for transfers between devices: 60.3 us -> none  [per_device(): lax.all_gather(weight_neigh, 'feat', axis=0, tiled=True)]
    all_to_all x0 -> x2, blocking collectives: none -> 49.9 us  [the longest x1 34.8 us: per_device(): all_to_all(jnp.stack([weight_neigh] * axis_size('feat')), 'feat', 0, 0)]
    all_gather x1, waiting for transfers between devices: 7.15 us -> 0.01 us  [per_device(): lax.all_gather(weight_self, 'feat', axis=0, tiled=True)]
    all_gather x1, waiting for transfers between devices: 67.5 us -> 61.1 us  [per_device(): shard_piece = lax.all_gather(grad_pre, 'feat', axis=0, tiled=True)]
    all_to_all x1 -> x0, starting transfers between devices: 5.62 us -> none  [per_device(): lax.all_to_all(aggregate, 'feat', split_axis=1, concat_axis=0, tiled=True)]
  transfers between devices with their start and end apart: 8 -> 6, of which waited for: 6 -> 4; matrix products, arithmetic and copies ran while one was open for 7% -> 6% of each run, Pallas kernels for 0% -> 0%
where the time goes in v1:
time: 382 us; the launch traced here: 381 us
  waiting for transfers between devices  183 us (48%)
  blocking collectives  100 us (26%)
  starting transfers between devices  34 us (9%)
  matrix products  32.9 us (9%)
  between operations  14.7 us (4%)
  local copies, waits for them, and re-layouts  11.2 us (3%)
  other arithmetic  5.43 us (1%)
    psum x1, waiting for transfers between devices, per_device(): lax.psum((grad_w_self, grad_w_neigh, bias_term), 'dom')  100 us
    all_gather x1, waiting for transfers between devices, per_device(): shard_piece = lax.all_gather(grad_pre, 'feat', axis=0, tiled=True)  61.1 us
    psum x1, blocking collectives, per_device(): lax.psum((grad_w_self, grad_w_neigh, bias_term), 'dom')  35.6 us
    all_to_all x1, blocking collectives, per_device(): all_to_all(jnp.stack([weight_neigh] * axis_size('feat')), 'feat', 0, 0)  34.8 us
    all_to_all x1, waiting for transfers between devices, per_device(): lax.all_to_all(outgoing, 'dom', split_axis=1, concat_axis=1, tiled=True)  16.2 us
    all_to_all x1, starting transfers between devices, per_device(): lax.all_to_all(outgoing, 'dom', split_axis=1, concat_axis=1, tiled=True)  15.2 us
    all_to_all x1, blocking collectives, per_device(): lax.all_to_all(aggregate, 'feat', split_axis=1, concat_axis=0, tiled=True)  15.1 us
    all_to_all x1, blocking collectives, per_device(): lax.all_to_all(out_by_rows, 'feat', split_axis=0, concat_axis=1, tiled=True)  14.5 us
  transfers between devices with their start and end apart: 6, of which 4 were waited for; matrix products, arithmetic and copies ran while one was open for 6% of the time, Pallas kernels for 0%

profile of v1, /device:TPU:2, one launch (start us, length us, event | category | flops | bytes accessed | tf_op | source)
XLA Modules:
  0.0 381.2 jit_solution(14127530618066815586)
XLA Ops:
  7.2 0.9 copy.39
  8.2 0.7 copy_bitcast_fusion.1
  9.0 1.5 gather_fusion
  10.8 0.8 copy.42
  11.5 15.2 %all-to-all-start.1 = ((bf16[32,16,256]{2,0,1:T(8,128)(2,1)}), bf16[32,16,256]{2,0,1:T(8,128)(2,1)S(1)}, u32[]{:S(2)}, u32[]{:S(2)}) async-start(bf16[32,16,256]{2,0,1:T(8,128)(2,1)} %copy.42), calls=%async_computation.1 | async-start | bytes 524288 | tf_op jit(solution)/shard_map/all_to_all | solution.py:47
  26.8 0.7 all-gather.3.cloned.1.call-update
  29.0 16.2 %all-to-all-done.1 = bf16[32,16,256]{2,0,1:T(8,128)(2,1)S(1)} async-done(((bf16[32,16,256]{2,0,1:T(8,128)(2,1)}), bf16[32,16,256]{2,0,1:T(8,128)(2,1)S(1)}, u32[]{:S(2)}, u32[]{:S(2)}) %all-to-all-start.1) | async-done | bytes 262176 | tf_op jit(solution)/shard_map/all_to_all | solution.py:47
  45.5 1.0 pad_maximum_fusion
  47.2 1.2 fusion.6
  48.3 1.2 fusion.16
  50.3 15.1 %all_to_all.74 = bf16[32,32,128]{2,0,1:T(8,128)(2,1)S(1)} all-to-all(bf16[32,32,128]{2,0,1:T(8,128)(2,1)S(1)} %copy.47), channel_id=1, replica_groups=mesh['dom'=16,'feat'=32] {'feat'}, dimensions={1} | all-to-all | bytes 524288 | tf_op jit(solution)/shard_map/all_to_all | solution.py:62
  65.7 34.8 %all_to_all.75 = bf16[32,32,1024]{2,1,0:T(8,128)(2,1)} all-to-all(bf16[32,32,1024]{2,1,0:T(8,128)(2,1)S(1)} %stack.2), channel_id=1, replica_groups=mesh['dom'=16,'feat'=32] {'feat'}, dimensions={0} | all-to-all | bytes 4194304 | tf_op jit(solution)/shard_map/all_to_all | solution.py:67
  100.4 6.4 %all-to-all-start = ((bf16[32,32,128]{2,0,1:T(8,128)(2,1)}), bf16[32,32,128]{2,0,1:T(8,128)(2,1)S(1)}, u32[]{:S(2)}, u32[]{:S(2)}) async-start(bf16[32,32,128]{2,0,1:T(8,128)(2,1)} %copy_bitcast_fusion.1), calls=%async_computation | async-start | bytes 524288 | tf_op jit(solution)/shard_map/all_to_all | solution.py:61
  106.9 3.1 fusion.12
  110.0 4.5 %all-to-all-done = bf16[32,32,128]{2,0,1:T(8,128)(2,1)S(1)} async-done(((bf16[32,32,128]{2,0,1:T(8,128)(2,1)}), bf16[32,32,128]{2,0,1:T(8,128)(2,1)S(1)}, u32[]{:S(2)}, u32[]{:S(2)}) %all-to-all-start) | async-done | bytes 262176 | tf_op jit(solution)/shard_map/all_to_all | solution.py:61
  114.5 2.4 convolution_add_fusion
  116.9 14.5 %all_to_all.76 = f32[32,32,128]{2,1,0:T(8,128)S(1)} all-to-all(f32[32,32,128]{2,1,0:T(8,128)S(1)} %bitcast.117), channel_id=1, replica_groups=mesh['dom'=16,'feat'=32] {'feat'}, dimensions={0} | all-to-all | bytes 1048576 | tf_op jit(solution)/shard_map/all_to_all | solution.py:71
  131.4 1.4 convert_reduce_fusion.1
  132.9 61.1 %all-gather.5.cloned.1.call-done = bf16[1024,4096]{1,0:T(8,128)(2,1)} async-done(((bf16[32,4096]{1,0:T(8,128)(2,1)}), bf16[1024,4096]{1,0:T(8,128)(2,1)}) %all-gather.5.cloned.1.call-update) | async-done | bytes 8388624 | tf_op jit(solution)/shard_map/all_gather | solution.py:77
  194.0 5.1 %convolution_bitcast_fusion.1 = f32[4,32,8,128]{3,2,1,0:T(8,128)S(1)} fusion(bf16[32,1024]{1,0:T(8,128)(2,1)S(1)} %copy-done.5, bf16[1024,4096]{1,0:T(8,128)(2,1)} %all-gather.5.cloned.1.call-done), kind=kOutput, calls=%fused_computation.14 | convolution fusion | flops 268435456 | bytes 8978432 | tf_op jit(solution)/shard_map/dot_general | solution.py:87
  199.7 1.5 convolution_bitcast_fusion.2
  201.4 1.7 gather_fusion.2
  203.1 3.0 fusion.9
  206.0 1.6 convolution_bitcast_fusion
  207.9 1.1 copy.55
  209.1 12.3 %all-to-all-start.5 = ((f32[32,16,256]{2,0,1:T(8,128)}), f32[32,16,256]{2,0,1:T(8,128)S(1)}, u32[]{:S(2)}, u32[]{:S(2)}) async-start(f32[32,16,256]{2,0,1:T(8,128)} %copy.55), calls=%async_computation.5 | async-start | bytes 1048576 | tf_op jit(solution)/shard_map/all_to_all | solution.py:108
  221.4 6.7 %convolution_bitcast_fusion.4 = f32[32,1024]{1,0:T(8,128)} fusion(bf16[1024,4096]{1,0:T(8,128)(2,1)} %all-gather.5.cloned.1.call-done, bf16[32,4096]{1,0:T(8,128)(2,1)S(1)} %copy-done), kind=kOutput, calls=%fused_computation.22 | convolution fusion | flops 268435456 | bytes 8781824 | tf_op jit(solution)/shard_map/dot_general | solution.py:78
  228.1 6.6 %fusion.32 = f32[32,1024]{1,0:T(8,128)} fusion(bf16[1024,4096]{1,0:T(8,128)(2,1)} %all-gather.5.cloned.1.call-done, bf16[4,8,32,128]{3,2,1,0:T(8,128)(2,1)S(1)} %bitcast.119), kind=kOutput, calls=%fused_computation.48 | convolution fusion | flops 268435456 | bytes 8781824 | tf_op jit(solution)/shard_map/dot_general | solution.py:81
  234.8 35.6 %psum.23 = f32[32]{0:T(128)S(1)} all-reduce(f32[32]{0:T(128)S(1)} %get-tuple-element.7), channel_id=1, replica_groups=mesh['dom'=16,'feat'=32] {'dom'}, use_global_device_ids=true, to_apply=%region_4.5 | all-reduce | flops 32 | bytes 256 | tf_op jit(solution)/shard_map/psum | solution.py:96
  271.0 100.4 %all-reduce.3.cloned.1.call-done = (f32[32,1024]{1,0:T(8,128)}, f32[32,1024]{1,0:T(8,128)}) async-done(((f32[32,1024]{1,0:T(8,128)}, f32[32,1024]{1,0:T(8,128)}), (f32[32,1024]{1,0:T(8,128)}, f32[32,1024]{1,0:T(8,128)})) %all-reduce.3.cloned.1.call-update) | async-done | bytes 262160 | tf_op jit(solution)/shard_map/psum | solution.py:96
  371.4 1.7 broadcast_multiply_fusion
  373.9 0.8 copy.96
  (56 shorter events, 5.6 us)
Async XLA Ops:
  7.2 1.1 copy-start
  7.2 21.0 %copy-start.10 = (s32[1,64]{1,0:T(1,128)S(1)}, s32[1,64]{1,0:T(1,128)}, u32[]{:S(2)}) copy-start(s32[1,64]{1,0:T(1,128)} %param.17) | copy-start | bytes 772
  7.2 21.0 %copy-start.2 = (bf16[1,64,128,128]{3,2,1,0:T(8,128)(2,1)S(1)}, bf16[1,64,128,128]{3,2,1,0:T(8,128)(2,1)}, u32[]{:S(2)}) copy-start(bf16[1,64,128,128]{3,2,1,0:T(8,128)(2,1)} %param.19) | copy-start | bytes 6291460
  10.5 18.3 %copy-start.9 = (s32[1,64]{1,0:T(1,128)S(1)}, s32[1,64]{1,0:T(1,128)}, u32[]{:S(2)}) copy-start(s32[1,64]{1,0:T(1,128)} %param.16) | copy-start | bytes 772
  11.5 33.6 %all-to-all-start.1 = ((bf16[32,16,256]{2,0,1:T(8,128)(2,1)}), bf16[32,16,256]{2,0,1:T(8,128)(2,1)S(1)}, u32[]{:S(2)}, u32[]{:S(2)}) async-start(bf16[32,16,256]{2,0,1:T(8,128)(2,1)} %copy.42), calls=%async_computation.1 | async-start | bytes 524288 | tf_op jit(solution)/shard_map/all_to_all | solution.py:47
  26.7 87.8 %all-gather.3.cloned.1.call-start = ((), (), s32[]{:S(2)}) async-start(), calls=%async_computation.6 | async-start | bytes 2162688 | tf_op jit(solution)/shard_map/all_gather | solution.py:64
  48.3 17.1 %copy-start.5 = (bf16[32,1024]{1,0:T(8,128)(2,1)S(1)}, bf16[32,1024]{1,0:T(8,128)(2,1)}, u32[]{:S(2)}) copy-start(bf16[32,1024]{1,0:T(8,128)(2,1)} %param.13) | copy-start | bytes 196612
  49.6 0.7 copy-start.3
  100.4 14.1 %all-to-all-start = ((bf16[32,32,128]{2,0,1:T(8,128)(2,1)}), bf16[32,32,128]{2,0,1:T(8,128)(2,1)S(1)}, u32[]{:S(2)}, u32[]{:S(2)}) async-start(bf16[32,32,128]{2,0,1:T(8,128)(2,1)} %copy_bitcast_fusion.1), calls=%async_computation | async-start | bytes 524288 | tf_op jit(solution)/shard_map/all_to_all | solution.py:61
  106.8 87.1 %all-gather.5.cloned.1.call-start = ((), (), s32[]{:S(2)}) async-start(), calls=%async_computation.7 | async-start | bytes 8650752 | tf_op jit(solution)/shard_map/all_gather | solution.py:77
  114.5 16.9 %copy-start.7 = (bf16[32,4096]{1,0:T(8,128)(2,1)S(1)}, bf16[32,4096]{1,0:T(8,128)(2,1)}, u32[]{:S(2)}) copy-start(bf16[32,4096]{1,0:T(8,128)(2,1)} %param.11) | copy-start | bytes 786436
  114.5 16.9 %copy-start.8 = (f32[32]{0:T(128)S(1)}, f32[32]{0:T(128)}, u32[]{:S(2)}) copy-start(f32[32]{0:T(128)} %param.14) | copy-start | bytes 388
  132.9 66.2 %copy-start.6 = (bf16[32,1024]{1,0:T(8,128)(2,1)S(1)}, bf16[32,1024]{1,0:T(8,128)(2,1)}, u32[]{:S(2)}) copy-start(bf16[32,1024]{1,0:T(8,128)(2,1)} %param.12) | copy-start | bytes 196612
  194.0 5.8 %copy-start.1 = (bf16[1024,4096]{1,0:T(8,128)(2,1)S(1)}, bf16[1024,4096]{1,0:T(8,128)(2,1)}, u32[]{:S(2)}) copy-start(bf16[1024,4096]{1,0:T(8,128)(2,1)} %all-gather.5.cloned.1.call-done) | copy-start | bytes 25165828
  209.1 164.0 %all-to-all-start.5 = ((f32[32,16,256]{2,0,1:T(8,128)}), f32[32,16,256]{2,0,1:T(8,128)S(1)}, u32[]{:S(2)}, u32[]{:S(2)}) async-start(f32[32,16,256]{2,0,1:T(8,128)} %copy.55), calls=%async_computation.5 | async-start | bytes 1048576 | tf_op jit(solution)/shard_map/all_to_all | solution.py:108
  221.4 6.7 %copy-start.4 = (bf16[32,32,128]{2,0,1:T(8,128)(2,1)S(1)}, bf16[32,32,128]{2,0,1:T(8,128)(2,1)}, u32[]{:S(2)}) copy-start(bf16[32,32,128]{2,0,1:T(8,128)(2,1)} %copy-done.3) | copy-start | bytes 786436
  221.4 150.0 %all-reduce.3.cloned.1.call-start = ((), (), s32[]{:S(2)}) async-start(), calls=%async_computation.8 | async-start | bytes 524288 | tf_op jit(solution)/shard_map/psum | solution.py:96
Sparse Core Ops, SparseCore 0:
  30.7 70.0 all-gather.2
  133.0 60.9 all-gather.4
  234.9 136.5 all-reduce.2
